TPU v7x, 256 devices: a whole 4x4x8 slice. The times are simulated.
256 devices in a mesh: seq: 32 (over x, y, core), tp: 8 (over z).
Axes of the slice: x: 4, y: 4, z: 8, core: 2. Of those that a mesh axis runs over, the one named last changes fastest.
Arguments:
- queries: bfloat16 [49152, 4096], P(('seq', 'tp')), may hold values from -9 to 9
- keys_values: bfloat16 [49152, 2048], P(('seq', 'tp')), may hold values from -8 to 8
- doc_lengths: int32 [32], replicated, may hold values from 1 to 3072, 49152 in all
- block_target: int32 [384], replicated, may hold values from 0 to 31, as said below
Outputs:
- attention_output: bfloat16 [49152, 4096], P('seq', 'tp')
Inputs may be any that keep to these rules, and one draw needn't show every extreme that they name: `doc_lengths`: the lengths add up to 49152, and the largest is exactly 3072. `block_target`: every shard of seq is named by exactly 12 blocks, and the 12 blocks of one shard of seq (blocks k * 12 to k * 12 + 11) name no shard more than 1 times, some shard exactly 1 times.
All inputs are finite; a program needn't handle non-finite values.
Results may differ from a plain program's by a relative error of at most 0.0036.
Values may be sent and summed in bfloat16 or wider, within the bound.
A program may use at most 128 MiB of HBM per device.

v0:
```python
import functools
import math

import jax
import jax.numpy as jnp
from jax import lax
from jax.experimental import pallas as pl
from jax.experimental.pallas import tpu as pltpu
from jax.sharding import PartitionSpec as P

HEADS = 32
KV_HEADS = 8
HEAD = 128
BLOCK = 128
MAXDOC = 3072

MESH = pl.DeviceIdType.MESH
GROUP = HEADS // KV_HEADS
WIDTH = GROUP * HEAD
PAIR = 2 * HEAD
WINDOW = MAXDOC + BLOCK
TILE = 5 * BLOCK
TILES = WINDOW // TILE
COLS = 2 * HEAD
PIECE_ROWS = 8
PIECE_COLS = 256
ONES = 16
CONTRACT_LAST = (((1,), (1,)), ((), ()))
APART = -32768.0
SCALE = math.log2(math.e) / math.sqrt(HEAD)


def ring_order(n):
    order = []
    for d in range(1, n // 2 + 1):
        order.append(d)
        if n - d != d:
            order.append(n - d)
    return order


def document_features(starts, ends, first, rows, apart):
    position = first + lax.broadcasted_iota(jnp.int32, (rows, HEAD), 0)
    inside = (position >= starts) & (position < ends)
    if apart:
        return jnp.where(inside, 0.0, APART).astype(jnp.bfloat16)
    return jnp.where(inside, 1.0, 0.0).astype(jnp.bfloat16)


def whole_kernel(
    n_tp, n_seq, rows,
    order_ref, starts_ref, ends_ref, q_ref, kv_ref, out_ref,
    pairs, q_here, key_aug, value_t, query_aug, scores_a, scores_b, top_a, top_b, attended, middle, outgoing,
    kv_send, kv_recv, q_send, q_recv, h_send, h_recv, send1, recv1, send2, recv2, own_sem,
):
    me = lax.axis_index("tp")
    shard = lax.axis_index("seq")
    shard_rows = n_tp * rows
    halo = MAXDOC // shard_rows
    slots = shard_rows // BLOCK
    groups = n_tp // 2
    per_group = slots // groups
    my_group = me // 2
    base = shard * shard_rows - MAXDOC
    near = ring_order(n_tp)
    far = ring_order(n_seq)
    starts, ends = starts_ref[...], ends_ref[...]

    barrier = pltpu.get_barrier_semaphore()
    for d in near:
        pl.semaphore_signal(barrier, inc=1, device_id={"tp": lax.rem(me + d, n_tp)}, device_id_type=MESH)
    for d in far:
        pl.semaphore_signal(barrier, inc=1, device_id={"seq": lax.rem(shard + d, n_seq)}, device_id_type=MESH)
    pl.semaphore_wait(barrier, n_tp - 1 + n_seq - 1)

    def columns(ref, which, width):
        return ref.at[:, pl.ds(pl.multiple_of(which * width, width), width)]

    def token_rows(ref, first, which):
        return ref.at[pl.ds(pl.multiple_of(first + which * rows, 64), rows), :]

    own_kv = pltpu.make_async_copy(columns(kv_ref, me, PAIR), token_rows(pairs, MAXDOC, me), own_sem.at[0])
    own_q = pltpu.make_async_copy(columns(q_ref, me, WIDTH), token_rows(q_here, 0, me), own_sem.at[1])
    own_kv.start()
    kv_copies = {}
    for d in near:
        peer = lax.rem(me + d, n_tp)
        kv_copies[d] = pltpu.make_async_remote_copy(
            src_ref=columns(kv_ref, peer, PAIR),
            dst_ref=token_rows(pairs, MAXDOC, me),
            send_sem=kv_send.at[d],
            recv_sem=kv_recv.at[d],
            device_id={"tp": peer},
            device_id_type=MESH,
        )
        kv_copies[d].start()

    def q_copy(peer, send, receive):
        return pltpu.make_async_remote_copy(
            src_ref=columns(q_ref, peer, WIDTH),
            dst_ref=token_rows(q_here, 0, me),
            send_sem=q_send.at[send],
            recv_sem=q_recv.at[receive],
            device_id={"tp": peer},
            device_id_type=MESH,
        )

    own_q.start()
    partner = me + 1 - 2 * (me % 2)
    q_copies = [q_copy(partner, 1, 1)]
    for k in range(1, groups):
        group = lax.rem(my_group + groups - k, groups)
        for i in range(2):
            q_copies.append(q_copy(2 * group + i, 2 * k + i, 2 * k + me % 2))
    for copy in q_copies:
        copy.start()

    @pl.loop(0, pairs.shape[0] // BLOCK)
    def _(i):
        at = pl.multiple_of(i * BLOCK, BLOCK)
        key_aug[pl.ds(at, BLOCK), HEAD:] = document_features(starts, ends, base + at, BLOCK, True)
        value_t[HEAD:, pl.ds(at, BLOCK)] = jnp.ones((ONES, BLOCK), jnp.bfloat16)

    def relay(d, h):
        origin = lax.rem(me + n_tp - d, n_tp)
        return pltpu.make_async_remote_copy(
            src_ref=token_rows(pairs, MAXDOC, origin),
            dst_ref=token_rows(pairs, MAXDOC - h * shard_rows, origin),
            send_sem=h_send.at[h - 1, d],
            recv_sem=h_recv.at[h - 1, d],
            device_id={"seq": lax.rem(shard + h, n_seq)},
            device_id_type=MESH,
        )

    own_kv.wait()
    for h in range(1, halo + 1):
        relay(0, h).start()
    for d in near:
        kv_copies[d].wait_recv()
        for h in range(1, halo + 1):
            relay(d, h).start()

    def prepare(first, count):
        @pl.loop(0, count)
        def _(i):
            at = pl.multiple_of(first + i * BLOCK, BLOCK)
            here = pl.ds(at, BLOCK)
            key_aug[here, :HEAD] = pairs[here, :HEAD]
            value_t[:HEAD, here] = pairs[here, HEAD:].astype(jnp.float32).T.astype(jnp.bfloat16)

    prepare(MAXDOC, slots)
    for h in range(1, halo + 1):
        for d in [0] + near:
            relay(d, h).wait_recv()
        prepare(MAXDOC - h * shard_rows, slots)

    def score_tile(block, local, half, i, scores, top):
        at = pl.multiple_of(block * BLOCK + i * TILE, BLOCK)
        tile = lax.dot_general(
            key_aug[pl.ds(at, TILE), :], query_aug[local, half * COLS:(half + 1) * COLS, :], CONTRACT_LAST,
            preferred_element_type=jnp.float32,
        )
        if i == TILES - 1:
            key_pos = lax.broadcasted_iota(jnp.int32, (BLOCK, COLS), 0)
            query_pos = lax.broadcasted_iota(jnp.int32, (BLOCK, COLS), 1) % BLOCK
            last = jnp.where(key_pos <= query_pos, tile[-BLOCK:], APART)
            tile = jnp.concatenate([tile[:-BLOCK], last], axis=0)
        scores[i * TILE:(i + 1) * TILE, :] = tile
        best = jnp.max(tile.reshape(TILE // 8, 8, COLS), axis=0)
        return best if top is None else jnp.maximum(top, best)

    def weigh_tile(block, i, scores, top, total):
        at = pl.multiple_of(block * BLOCK + i * TILE, BLOCK)
        weights = jnp.exp2(scores[i * TILE:(i + 1) * TILE, :] * SCALE - top).astype(jnp.bfloat16)
        part = jnp.dot(value_t[:, pl.ds(at, TILE)], weights, preferred_element_type=jnp.float32)
        return part if total is None else total + part

    def finish(block, half, total):
        result = total[:HEAD] * (1.0 / total[HEAD:HEAD + 1])
        for h in range(COLS // BLOCK):
            head = result[:, h * BLOCK:(h + 1) * BLOCK].T.reshape(BLOCK // PIECE_ROWS, PIECE_ROWS, HEAD)
            at = half * COLS + h * HEAD
            attended[block, :, :, at:at + HEAD] = head.astype(jnp.bfloat16)

    buffers = ((scores_a, top_a), (scores_b, top_b))

    def overlap(ahead, behind):
        top = None
        if behind is not None:
            block, _, half = behind
            limit = jnp.max(buffers[half][1][...], axis=0, keepdims=True) * SCALE
        total = None
        for i in range(TILES):
            if ahead is not None:
                top = score_tile(*ahead, i, buffers[ahead[2]][0], top)
            if behind is not None:
                total = weigh_tile(block, i, buffers[half][0], limit, total)
        if ahead is not None:
            buffers[ahead[2]][1][...] = top
        if behind is not None:
            finish(block, half, total)

    def piece(which):
        halves = WIDTH // PIECE_COLS
        return which // halves, pl.ds(pl.multiple_of((which % halves) * PIECE_COLS, PIECE_COLS), PIECE_COLS)

    def first_hop(k, d, group):
        peer = lax.rem(shard + d, n_seq)
        row, cols = piece(peer)
        return pltpu.make_async_remote_copy(
            src_ref=attended.at[pl.ds(group * per_group, per_group), row, :, cols],
            dst_ref=middle.at[pl.ds(shard * slots + group * per_group, per_group)],
            send_sem=send1.at[k, d],
            recv_sem=recv1.at[k, d],
            device_id={"seq": peer},
            device_id_type=MESH,
        )

    def own_hop(k, group):
        row, cols = piece(shard)
        return pltpu.make_async_copy(
            attended.at[pl.ds(group * per_group, per_group), row, :, cols],
            middle.at[pl.ds(shard * slots + group * per_group, per_group)],
            own_sem.at[2 + k],
        )

    @pl.loop(0, groups)
    def _(k):
        group = lax.rem(my_group + k, groups)

        @pl.when(k == 0)
        def _():
            own_q.wait()

        @pl.when(k > 0)
        def _():
            q_copy(partner, 2 * k, 2 * k).wait_recv()

        q_copy(partner, 2 * k + 1, 2 * k + 1).wait_recv()
        for local in range(per_group):
            at = pl.multiple_of((group * per_group + local) * BLOCK, BLOCK)
            features = document_features(starts, ends, base + MAXDOC + at, BLOCK, False)
            for h in range(GROUP):
                here = slice(h * BLOCK, (h + 1) * BLOCK)
                query_aug[local, here, :HEAD] = q_here[pl.ds(at, BLOCK), h * HEAD:(h + 1) * HEAD]
                query_aug[local, here, HEAD:] = features

        first = group * per_group
        overlap((first, 0, 0), None)

        @pl.loop(0, per_group - 1)
        def _(local):
            block = first + local
            overlap((block, local, 1), (block, local, 0))
            overlap((block + 1, local + 1, 0), (block, local, 1))

        last = first + per_group - 1
        overlap((last, per_group - 1, 1), (last, per_group - 1, 0))
        overlap(None, (last, per_group - 1, 1))

        own_hop(k, group).start()

        @pl.loop(1, n_seq)
        def _(d):
            first_hop(k, d, group).start()

    @pl.loop(0, groups)
    def _(k):
        own_hop(k, k).wait()

        @pl.loop(1, n_seq)
        def _(d):
            first_hop(k, d, k).wait_recv()

    def permute(which):
        for i in range(slots):
            row = which * slots + i
            outgoing[row] = middle[order_ref[row]]

    def second_hop(d):
        peer = lax.rem(shard + d, n_seq)
        row, cols = piece(shard)
        return pltpu.make_async_remote_copy(
            src_ref=outgoing.at[pl.ds(peer * slots, slots)],
            dst_ref=out_ref.at[:, pl.ds(pl.multiple_of(row * PIECE_ROWS, PIECE_ROWS), PIECE_ROWS), cols],
            send_sem=send2.at[d],
            recv_sem=recv2.at[d],
            device_id={"seq": peer},
            device_id_type=MESH,
        )

    @pl.loop(1, n_seq)
    def _(d):
        permute(lax.rem(shard + d, n_seq))
        second_hop(d).start()

    permute(shard)
    row, cols = piece(shard)
    home = pltpu.make_async_copy(
        outgoing.at[pl.ds(shard * slots, slots)],
        out_ref.at[:, pl.ds(pl.multiple_of(row * PIECE_ROWS, PIECE_ROWS), PIECE_ROWS), cols],
        own_sem.at[0],
    )
    home.start()
    for d in near:
        kv_copies[d].wait_send()
    for copy in q_copies:
        copy.wait_send()
    for h in range(1, halo + 1):
        for d in [0] + near:
            relay(d, h).wait_send()

    @pl.loop(0, groups)
    def _(k):
        @pl.loop(1, n_seq)
        def _(d):
            first_hop(k, d, k).wait_send()

    home.wait()

    @pl.loop(1, n_seq)
    def _(d):
        second_hop(d).wait()


def body(queries, keys_values, doc_lengths, block_target):
    n_seq, n_tp = lax.axis_size("seq"), lax.axis_size("tp")
    rows = queries.shape[0]
    shard_rows = n_tp * rows
    slots = shard_rows // BLOCK
    halo = MAXDOC // shard_rows
    groups = n_tp // 2
    blocks = n_seq * slots
    window_rows = MAXDOC + shard_rows

    ends = jnp.cumsum(doc_lengths)
    starts = ends - doc_lengths
    pad = HEAD - starts.shape[0]
    starts_row = jnp.pad(starts, (0, pad), constant_values=1 << 30)[None, :]
    ends_row = jnp.pad(ends, (0, pad), constant_values=1 << 30)[None, :]

    ids = jnp.arange(blocks, dtype=jnp.int32)
    earlier = (block_target[None, :] == block_target[:, None]) & (ids[None, :] < ids[:, None])
    place = block_target * slots + jnp.sum(earlier.astype(jnp.int32), axis=1)
    order = jnp.sum(jnp.where(place[None, :] == ids[:, None], ids[None, :], 0), axis=1).astype(jnp.int32)

    hbm = pl.BlockSpec(memory_space=pl.ANY)
    vmem = pl.BlockSpec(memory_space=pltpu.VMEM)
    dma = pltpu.SemaphoreType.DMA
    out = pl.pallas_call(
        functools.partial(whole_kernel, n_tp, n_seq, rows),
        out_shape=jax.ShapeDtypeStruct((slots, BLOCK, WIDTH), jnp.bfloat16),
        in_specs=[pl.BlockSpec(memory_space=pltpu.SMEM), vmem, vmem, hbm, hbm],
        out_specs=hbm,
        scratch_shapes=[
            pltpu.VMEM((window_rows, PAIR), jnp.bfloat16),
            pltpu.VMEM((shard_rows, WIDTH), jnp.bfloat16),
            pltpu.VMEM((window_rows, 2 * HEAD), jnp.bfloat16),
            pltpu.VMEM((HEAD + ONES, window_rows), jnp.bfloat16),
            pltpu.VMEM((slots // groups, WIDTH, 2 * HEAD), jnp.bfloat16),
            pltpu.VMEM((WINDOW, COLS), jnp.float32),
            pltpu.VMEM((WINDOW, COLS), jnp.float32),
            pltpu.VMEM((8, COLS), jnp.float32),
            pltpu.VMEM((8, COLS), jnp.float32),
            pltpu.VMEM((slots, BLOCK // PIECE_ROWS, PIECE_ROWS, WIDTH), jnp.bfloat16),
            pltpu.VMEM((blocks, PIECE_ROWS, PIECE_COLS), jnp.bfloat16),
            pltpu.VMEM((blocks, PIECE_ROWS, PIECE_COLS), jnp.bfloat16),
            dma((n_tp,)), dma((n_tp,)), dma((n_tp,)), dma((n_tp,)),
            dma((halo, n_tp)), dma((halo, n_tp)),
            dma((groups, n_seq)), dma((groups, n_seq)), dma((n_seq,)), dma((n_seq,)), dma((2 + groups,)),
        ],
        compiler_params=pltpu.CompilerParams(collective_id=0, has_side_effects=True, vmem_limit_bytes=56 << 20),
        name="attend_and_route",
    )(order, starts_row, ends_row, queries, keys_values)
    return out.reshape(shard_rows, WIDTH)


def solution(mesh):
    placed = (P(("seq", "tp"), None), P(("seq", "tp"), None), P(), P())
    return jax.shard_map(body, mesh=mesh, in_specs=placed, out_specs=P("seq", "tp"), check_vma=False)
```

profile of v0, /device:TPU:57, one launch (start us, length us, event | category | flops | bytes accessed | tf_op | source)
XLA Modules:
  0.0 122.1 jit_solution(8131498657605248974)
XLA Ops:
  0.0 1.0 convert_reduce_fusion
  1.0 0.7 multiply_add_fusion
  1.7 0.7 select_reduce_fusion.order_ref
  2.4 0.7 copy.7
  3.1 0.1 reduce-window.9
  3.2 0.1 reduce
  3.3 0.7 sub.3
  4.0 0.6 pad_bitcast_fusion
  4.6 114.9 %attend_and_route.1 = bf16[12,128,512]{2,1,0:T(8,128)(2,1)} custom-call(s32[384]{0:T(512)} %select_reduce_fusion.order_ref, s32[1,128]{1,0:T(1,128)} %get-tuple-element.6.starts_ref, s32[1,128]{1,0:T(1,128)} %get-tuple-element.5.ends_ref, bf16[192,4096]{1,0:T(8,128)(2,1)} %q_ref.1, bf16[192,2048]{1,0:T(8,128)(2,1)} %kv_ref.1), custom_call_target="tpu_custom_call" | custom-call | tf_op jit(solution)/shard_map/attend_and_route/pallas_call | solution.py:350
  119.5 2.7 %copy.9 = bf16[1536,512]{1,0:T(8,128)(2,1)} copy(bf16[1536,512]{1,0:T(8,128)(2,1)} %bitcast.6) | data formatting | bytes 3145728
where the time goes:
time: 122 us
  Pallas kernels  115 us (94%)
  local copies, waits for them, and re-layouts  3.97 us (3%)
  other arithmetic  3.24 us (3%)
    pallas_call x1, Pallas kernels, body(): pl.pallas_call(functools.partial(whole_kernel, n_tp, n_seq, rows), out_sh...  115 us
    unnamed x1, local copies, waits for them, and re-layouts  2.65 us

commit v1 on v0

--- a/solution.py
+++ b/solution.py
@@ -105,15 +105,12 @@
             device_id_type=MESH,
         )
 
-    own_q.start()
     partner = me + 1 - 2 * (me % 2)
     q_copies = [q_copy(partner, 1, 1)]
     for k in range(1, groups):
         group = lax.rem(my_group + groups - k, groups)
         for i in range(2):
             q_copies.append(q_copy(2 * group + i, 2 * k + i, 2 * k + me % 2))
-    for copy in q_copies:
-        copy.start()
 
     @pl.loop(0, pairs.shape[0] // BLOCK)
     def _(i):
@@ -135,10 +132,13 @@
     own_kv.wait()
     for h in range(1, halo + 1):
         relay(0, h).start()
-    for d in near:
+    for i, d in enumerate(near):
         kv_copies[d].wait_recv()
         for h in range(1, halo + 1):
             relay(d, h).start()
+        if i == 0:
+            own_q.start()
+        q_copies[i].start()
 
     def prepare(first, count):
         @pl.loop(0, count)

time: 122 us -> 122 us (level)
  no operation moved by 1% of the time
where the time goes in v1:
time: 122 us
  Pallas kernels  115 us (94%)
  local copies, waits for them, and re-layouts  3.97 us (3%)
  other arithmetic  3.24 us (3%)
    pallas_call x1, Pallas kernels, body(): pl.pallas_call(functools.partial(whole_kernel, n_tp, n_seq, rows), out_sh...  115 us
    unnamed x1, local copies, waits for them, and re-layouts  2.65 us

profile of v1, /device:TPU:57, one launch (start us, length us, event | category | flops | bytes accessed | tf_op | source)
XLA Modules:
  0.0 122.1 jit_solution(11655337124278640648)
XLA Ops:
  0.0 1.0 convert_reduce_fusion
  1.0 0.7 multiply_add_fusion
  1.7 0.7 select_reduce_fusion.order_ref
  2.4 0.7 copy.7
  3.1 0.1 reduce-window.9
  3.2 0.1 reduce
  3.3 0.7 sub.3
  4.0 0.6 pad_bitcast_fusion
  4.6 114.8 %attend_and_route.1 = bf16[12,128,512]{2,1,0:T(8,128)(2,1)} custom-call(s32[384]{0:T(512)} %select_reduce_fusion.order_ref, s32[1,128]{1,0:T(1,128)} %get-tuple-element.6.starts_ref, s32[1,128]{1,0:T(1,128)} %get-tuple-element.5.ends_ref, bf16[192,4096]{1,0:T(8,128)(2,1)} %q_ref.1, bf16[192,2048]{1,0:T(8,128)(2,1)} %kv_ref.1), custom_call_target="tpu_custom_call" | custom-call | tf_op jit(solution)/shard_map/attend_and_route/pallas_call | solution.py:350
  119.4 2.7 %copy.9 = bf16[1536,512]{1,0:T(8,128)(2,1)} copy(bf16[1536,512]{1,0:T(8,128)(2,1)} %bitcast.6) | data formatting | bytes 3145728

commit v2 on v1

v2 whole, which is shorter than its diff:
```python
import functools
import math

import jax
import jax.numpy as jnp
from jax import lax
from jax.experimental import pallas as pl
from jax.experimental.pallas import tpu as pltpu
from jax.sharding import PartitionSpec as P

HEADS = 32
KV_HEADS = 8
HEAD = 128
BLOCK = 128
MAXDOC = 3072

MESH = pl.DeviceIdType.MESH
GROUP = HEADS // KV_HEADS
WIDTH = GROUP * HEAD
PAIR = 2 * HEAD
WINDOW = MAXDOC + BLOCK
TILE = 5 * BLOCK
TILES = WINDOW // TILE
COLS = 2 * HEAD
PIECE_ROWS = 8
PIECE_COLS = 128
BATCHES = 2
ONES = 16
CONTRACT_LAST = (((1,), (1,)), ((), ()))
APART = -32768.0
SCALE = math.log2(math.e) / math.sqrt(HEAD)


def ring_order(n):
    order = []
    for d in range(1, n // 2 + 1):
        order.append(d)
        if n - d != d:
            order.append(n - d)
    return order


def document_features(starts, ends, first, rows, apart):
    position = first + lax.broadcasted_iota(jnp.int32, (rows, HEAD), 0)
    inside = (position >= starts) & (position < ends)
    if apart:
        return jnp.where(inside, 0.0, APART).astype(jnp.bfloat16)
    return jnp.where(inside, 1.0, 0.0).astype(jnp.bfloat16)


def whole_kernel(
    n_tp, n_seq, rows,
    order_ref, starts_ref, ends_ref, q_ref, kv_ref, out_ref,
    pairs, q_a, q_b, key_aug, value_t, query_aug, scores_a, scores_b, top_a, top_b, attended_a, attended_b, middle_a, middle_b, outgoing_a, outgoing_b,
    kv_send, kv_recv, q_send, q_recv, h_send, h_recv, send1, recv1, send2, recv2, own_sem,
):
    me = lax.axis_index("tp")
    shard = lax.axis_index("seq")
    shard_rows = n_tp * rows
    halo = MAXDOC // shard_rows
    slots = shard_rows // BLOCK
    groups = n_tp // 2
    per_group = slots // groups
    my_group = me // 2
    q_here = (q_a, q_b)
    base = shard * shard_rows - MAXDOC
    near = ring_order(n_tp)
    far = ring_order(n_seq)

    barrier = pltpu.get_barrier_semaphore()
    for d in near:
        pl.semaphore_signal(barrier, inc=1, device_id={"tp": lax.rem(me + d, n_tp)}, device_id_type=MESH)
    for d in far:
        pl.semaphore_signal(barrier, inc=1, device_id={"seq": lax.rem(shard + d, n_seq)}, device_id_type=MESH)
    pl.semaphore_wait(barrier, n_tp - 1 + n_seq - 1)

    def columns(ref, which, width):
        return ref.at[:, pl.ds(pl.multiple_of(which * width, width), width)]

    def token_rows(ref, first, which):
        return ref.at[pl.ds(pl.multiple_of(first + which * rows, 64), rows), :]

    own_kv = pltpu.make_async_copy(columns(kv_ref, me, PAIR), token_rows(pairs, MAXDOC, me), own_sem.at[0])
    own_kv.start()
    kv_copies = {}
    for d in near:
        peer = lax.rem(me + d, n_tp)
        kv_copies[d] = pltpu.make_async_remote_copy(
            src_ref=columns(kv_ref, peer, PAIR),
            dst_ref=token_rows(pairs, MAXDOC, me),
            send_sem=kv_send.at[d],
            recv_sem=kv_recv.at[d],
            device_id={"tp": peer},
            device_id_type=MESH,
        )
        kv_copies[d].start()

    partner = me + 1 - 2 * (me % 2)

    def kth_group(k):
        beside = my_group + (k % 2) * (1 - 2 * (my_group % 2))
        return lax.rem(beside + 2 * (k // 2), groups)

    def q_copy(batch, peer, send, receive):
        return pltpu.make_async_remote_copy(
            src_ref=q_ref.at[:, pl.ds(pl.multiple_of(peer * WIDTH + batch * COLS, COLS), COLS)],
            dst_ref=q_here[batch].at[pl.ds(pl.multiple_of(me * rows, 64), rows), :],
            send_sem=q_send.at[batch, send],
            recv_sem=q_recv.at[batch, receive],
            device_id={"tp": peer},
            device_id_type=MESH,
        )

    def send_queries(batch, k):
        for i in range(2):
            q_copy(batch, 2 * kth_group(k) + i, 2 * k + i, 2 * k + me % 2).start()

    def own_q(batch):
        return pltpu.make_async_copy(
            q_ref.at[:, pl.ds(pl.multiple_of(me * WIDTH + batch * COLS, COLS), COLS)],
            q_here[batch].at[pl.ds(pl.multiple_of(me * rows, 64), rows), :],
            own_sem.at[1 + batch],
        )

    starts, ends = starts_ref[...], ends_ref[...]

    @pl.loop(0, pairs.shape[0] // BLOCK)
    def _(i):
        at = pl.multiple_of(i * BLOCK, BLOCK)
        key_aug[pl.ds(at, BLOCK), HEAD:] = document_features(starts, ends, base + at, BLOCK, True)
        value_t[HEAD:, pl.ds(at, BLOCK)] = jnp.ones((ONES, BLOCK), jnp.bfloat16)

    def relay(d, h):
        origin = lax.rem(me + n_tp - d, n_tp)
        return pltpu.make_async_remote_copy(
            src_ref=token_rows(pairs, MAXDOC, origin),
            dst_ref=token_rows(pairs, MAXDOC - h * shard_rows, origin),
            send_sem=h_send.at[h - 1, d],
            recv_sem=h_recv.at[h - 1, d],
            device_id={"seq": lax.rem(shard + h, n_seq)},
            device_id_type=MESH,
        )

    own_kv.wait()
    for h in range(1, halo + 1):
        relay(0, h).start()
    for i, d in enumerate(near):
        kv_copies[d].wait_recv()
        for h in range(1, halo + 1):
            relay(d, h).start()
        if i == 1:
            own_q(0).start()
            q_copy(0, partner, 1, 1).start()
        elif i % 2:
            send_queries(0, i // 2)
    send_queries(0, groups - 1)

    def prepare(first, count):
        @pl.loop(0, count)
        def _(i):
            at = pl.multiple_of(first + i * BLOCK, BLOCK)
            here = pl.ds(at, BLOCK)
            key_aug[here, :HEAD] = pairs[here, :HEAD]
            value_t[:HEAD, here] = pairs[here, HEAD:].astype(jnp.float32).T.astype(jnp.bfloat16)

    prepare(MAXDOC, slots)
    for h in range(1, halo + 1):
        for d in [0] + near:
            relay(d, h).wait_recv()
        prepare(MAXDOC - h * shard_rows, slots)

    def score_tile(block, local, i, scores, top):
        at = pl.multiple_of(block * BLOCK + i * TILE, BLOCK)
        tile = lax.dot_general(
            key_aug[pl.ds(at, TILE), :], query_aug[local], CONTRACT_LAST, preferred_element_type=jnp.float32
        )
        if i == TILES - 1:
            key_pos = lax.broadcasted_iota(jnp.int32, (BLOCK, COLS), 0)
            query_pos = lax.broadcasted_iota(jnp.int32, (BLOCK, COLS), 1) % BLOCK
            last = jnp.where(key_pos <= query_pos, tile[-BLOCK:], APART)
            tile = jnp.concatenate([tile[:-BLOCK], last], axis=0)
        scores[i * TILE:(i + 1) * TILE, :] = tile
        best = jnp.max(tile.reshape(TILE // 8, 8, COLS), axis=0)
        return best if top is None else jnp.maximum(top, best)

    def weigh_tile(block, i, scores, top, total):
        at = pl.multiple_of(block * BLOCK + i * TILE, BLOCK)
        weights = jnp.exp2(scores[i * TILE:(i + 1) * TILE, :] * SCALE - top).astype(jnp.bfloat16)
        part = jnp.dot(value_t[:, pl.ds(at, TILE)], weights, preferred_element_type=jnp.float32)
        return part if total is None else total + part

    def finish(batch, block, total):
        result = total[:HEAD] * (1.0 / total[HEAD:HEAD + 1])
        for h in range(COLS // HEAD):
            head = result[:, h * BLOCK:(h + 1) * BLOCK].T.reshape(BLOCK // PIECE_ROWS, PIECE_ROWS, HEAD)
            attended[batch][block, :, :, h * HEAD:(h + 1) * HEAD] = head.astype(jnp.bfloat16)

    buffers = ((scores_a, top_a), (scores_b, top_b))
    middle = (middle_a, middle_b)
    attended = (attended_a, attended_b)
    outgoing = (outgoing_a, outgoing_b)

    def overlap(batch, first, ahead, behind):
        top = total = None
        if behind is not None:
            behind_scores, behind_top = buffers[behind % 2]
            limit = jnp.max(behind_top[...], axis=0, keepdims=True) * SCALE
        for i in range(TILES):
            if ahead is not None:
                top = score_tile(first + ahead, ahead, i, buffers[ahead % 2][0], top)
            if behind is not None:
                total = weigh_tile(first + behind, i, behind_scores, limit, total)
        if ahead is not None:
            buffers[ahead % 2][1][...] = top
        if behind is not None:
            finish(batch, first + behind, total)

    def piece(which):
        parts = COLS // PIECE_COLS
        return which // parts, which % parts

    def piece_of(batch, which, first, count):
        row, col = piece(which)
        cols = pl.ds(pl.multiple_of(col * PIECE_COLS, PIECE_COLS), PIECE_COLS)
        return attended[batch].at[pl.ds(first, count), row, :, cols]

    def first_hop(batch, step, d, first, count):
        peer = lax.rem(shard + d, n_seq)
        return pltpu.make_async_remote_copy(
            src_ref=piece_of(batch, peer, first, count),
            dst_ref=middle[batch].at[pl.ds(shard * slots + first, count)],
            send_sem=send1.at[step, d],
            recv_sem=recv1.at[step, d],
            device_id={"seq": peer},
            device_id_type=MESH,
        )

    def own_hop(batch, step, first, count):
        return pltpu.make_async_copy(
            piece_of(batch, shard, first, count),
            middle[batch].at[pl.ds(shard * slots + first, count)],
            own_sem.at[1 + BATCHES + step],
        )

    def attend_group(batch, k):
        group = kth_group(k)
        first = group * per_group

        @pl.when(k == 0)
        def _():
            own_q(batch).wait()

        @pl.when(k > 0)
        def _():
            q_copy(batch, partner, 2 * k, 2 * k).wait_recv()

        q_copy(batch, partner, 2 * k + 1, 2 * k + 1).wait_recv()
        if batch + 1 < BATCHES:
            @pl.when(k == 0)
            def _():
                own_q(batch + 1).start()
                q_copy(batch + 1, partner, 1, 1).start()

            @pl.when(k > 0)
            def _():
                send_queries(batch + 1, k)

        for local in range(per_group):
            at = pl.multiple_of((first + local) * BLOCK, BLOCK)
            features = document_features(starts, ends, base + MAXDOC + at, BLOCK, False)
            for h in range(COLS // HEAD):
                here = slice(h * BLOCK, (h + 1) * BLOCK)
                query_aug[local, here, :HEAD] = q_here[batch][pl.ds(at, BLOCK), h * HEAD:(h + 1) * HEAD]
                query_aug[local, here, HEAD:] = features

        for unit in range(per_group + 1):
            overlap(batch, first, unit if unit < per_group else None, unit - 1 if unit else None)

    def permute(batch, which):
        for i in range(slots):
            row = which * slots + i
            outgoing[batch][row] = middle[batch][order_ref[row]]

    def out_piece(batch):
        row, col = piece(shard)
        return out_ref.at[
            :,
            pl.ds(pl.multiple_of(row * PIECE_ROWS, PIECE_ROWS), PIECE_ROWS),
            pl.ds(pl.multiple_of(batch * COLS + col * PIECE_COLS, PIECE_COLS), PIECE_COLS),
        ]

    def second_hop(batch, d):
        peer = lax.rem(shard + d, n_seq)
        return pltpu.make_async_remote_copy(
            src_ref=outgoing[batch].at[pl.ds(peer * slots, slots)],
            dst_ref=out_piece(batch),
            send_sem=send2.at[batch, d],
            recv_sem=recv2.at[batch, d],
            device_id={"seq": peer},
            device_id_type=MESH,
        )

    def home(batch):
        return pltpu.make_async_copy(outgoing[batch].at[pl.ds(shard * slots, slots)], out_piece(batch), own_sem.at[0])

    def second_phase(batch):
        @pl.loop(1, n_seq)
        def _(d):
            permute(batch, lax.rem(shard + d, n_seq))
            second_hop(batch, d).start()

        permute(batch, shard)
        home(batch).start()
        home(batch).wait()

    def first_phase(batch, k):
        first = kth_group(k) * per_group
        step = batch * groups + k
        own_hop(batch, step, first, per_group).start()

        @pl.loop(1, n_seq)
        def _(d):
            first_hop(batch, step, d, first, per_group).start()

    def arrived(batch):
        @pl.loop(0, groups)
        def _(k):
            own_hop(batch, batch * groups + k, k * per_group, per_group).wait()

            @pl.loop(1, n_seq)
            def _(d):
                first_hop(batch, batch * groups + k, d, k * per_group, per_group).wait_recv()

    @pl.loop(0, groups)
    def _(k):
        attend_group(0, k)
        first_phase(0, k)

    @pl.loop(0, 1)
    def _(k):
        attend_group(1, k)
        first_phase(1, k)

    arrived(0)
    second_phase(0)

    @pl.loop(1, groups)
    def _(k):
        attend_group(1, k)
        first_phase(1, k)

    arrived(1)
    second_phase(1)

    for d in near:
        kv_copies[d].wait_send()
    for h in range(1, halo + 1):
        for d in [0] + near:
            relay(d, h).wait_send()
    for batch in range(BATCHES):
        for i in range(1, n_tp):
            q_copy(batch, partner, i, i).wait_send()

    @pl.loop(0, groups)
    def _(k):
        @pl.loop(1, n_seq)
        def _(d):
            for batch in range(BATCHES):
                first_hop(batch, batch * groups + k, d, k * per_group, per_group).wait_send()

    @pl.loop(1, n_seq)
    def _(d):
        for batch in range(BATCHES):
            second_hop(batch, d).wait()


def body(queries, keys_values, doc_lengths, block_target):
    n_seq, n_tp = lax.axis_size("seq"), lax.axis_size("tp")
    rows = queries.shape[0]
    shard_rows = n_tp * rows
    slots = shard_rows // BLOCK
    halo = MAXDOC // shard_rows
    groups = n_tp // 2
    blocks = n_seq * slots
    window_rows = MAXDOC + shard_rows

    ends = jnp.cumsum(doc_lengths)
    starts = ends - doc_lengths
    pad = HEAD - starts.shape[0]
    starts_row = jnp.pad(starts, (0, pad), constant_values=1 << 30)[None, :]
    ends_row = jnp.pad(ends, (0, pad), constant_values=1 << 30)[None, :]

    ids = jnp.arange(blocks, dtype=jnp.int32)
    earlier = (block_target[None, :] == block_target[:, None]) & (ids[None, :] < ids[:, None])
    place = block_target * slots + jnp.sum(earlier.astype(jnp.int32), axis=1)
    order = jnp.sum(jnp.where(place[None, :] == ids[:, None], ids[None, :], 0), axis=1).astype(jnp.int32)

    hbm = pl.BlockSpec(memory_space=pl.ANY)
    vmem = pl.BlockSpec(memory_space=pltpu.VMEM)
    dma = pltpu.SemaphoreType.DMA
    out = pl.pallas_call(
        functools.partial(whole_kernel, n_tp, n_seq, rows),
        out_shape=jax.ShapeDtypeStruct((slots, BLOCK, WIDTH), jnp.bfloat16),
        in_specs=[pl.BlockSpec(memory_space=pltpu.SMEM), vmem, vmem, hbm, hbm],
        out_specs=hbm,
        scratch_shapes=[
            pltpu.VMEM((window_rows, PAIR), jnp.bfloat16),
            pltpu.VMEM((shard_rows, COLS), jnp.bfloat16),
            pltpu.VMEM((shard_rows, COLS), jnp.bfloat16),
            pltpu.VMEM((window_rows, 2 * HEAD), jnp.bfloat16),
            pltpu.VMEM((HEAD + ONES, window_rows), jnp.bfloat16),
            pltpu.VMEM((slots // groups, COLS, 2 * HEAD), jnp.bfloat16),
            pltpu.VMEM((WINDOW, COLS), jnp.float32),
            pltpu.VMEM((WINDOW, COLS), jnp.float32),
            pltpu.VMEM((8, COLS), jnp.float32),
            pltpu.VMEM((8, COLS), jnp.float32),
            pltpu.VMEM((slots, BLOCK // PIECE_ROWS, PIECE_ROWS, COLS), jnp.bfloat16),
            pltpu.VMEM((slots, BLOCK // PIECE_ROWS, PIECE_ROWS, COLS), jnp.bfloat16),
            pltpu.VMEM((blocks, PIECE_ROWS, PIECE_COLS), jnp.bfloat16),
            pltpu.VMEM((blocks, PIECE_ROWS, PIECE_COLS), jnp.bfloat16),
            pltpu.VMEM((blocks, PIECE_ROWS, PIECE_COLS), jnp.bfloat16),
            pltpu.VMEM((blocks, PIECE_ROWS, PIECE_COLS), jnp.bfloat16),
            dma((n_tp,)), dma((n_tp,)), dma((BATCHES, n_tp)), dma((BATCHES, n_tp)),
            dma((halo, n_tp)), dma((halo, n_tp)),
            dma((BATCHES * groups, n_seq)), dma((BATCHES * groups, n_seq)), dma((BATCHES, n_seq)), dma((BATCHES, n_seq)),
            dma((2 + BATCHES + BATCHES * groups,)),
        ],
        compiler_params=pltpu.CompilerParams(collective_id=0, has_side_effects=True, vmem_limit_bytes=56 << 20),
        name="attend_and_route",
    )(order, starts_row, ends_row, queries, keys_values)
    return out.reshape(shard_rows, WIDTH)


def solution(mesh):
    placed = (P(("seq", "tp"), None), P(("seq", "tp"), None), P(), P())
    return jax.shard_map(body, mesh=mesh, in_specs=placed, out_specs=P("seq", "tp"), check_vma=False)
```

time: 122 us -> 110 us (0.902)
  the two profiles are of different devices: /device:TPU:57 before, /device:TPU:25 now
where the time goes in v2:
time: 110 us; the launch traced here: 109 us
  Pallas kernels  102 us (93%)
  local copies, waits for them, and re-layouts  3.97 us (4%)
  other arithmetic  3.24 us (3%)
    pallas_call x1, Pallas kernels, body(): pl.pallas_call(functools.partial(whole_kernel, n_tp, n_seq, rows), out_sh...  102 us
    unnamed x1, local copies, waits for them, and re-layouts  2.65 us

profile of v2, /device:TPU:25, one launch (start us, length us, event | category | flops | bytes accessed | tf_op | source)
XLA Modules:
  0.0 109.3 jit_solution(16342294629420744672)
XLA Ops:
  0.0 1.0 convert_reduce_fusion
  1.0 0.7 multiply_add_fusion
  1.7 0.7 select_reduce_fusion.order_ref
  2.4 0.7 copy.7
  3.1 0.1 reduce-window.9
  3.2 0.1 reduce
  3.3 0.7 sub.3
  4.0 0.6 pad_bitcast_fusion
  4.6 102.1 %attend_and_route.1 = bf16[12,128,512]{2,1,0:T(8,128)(2,1)} custom-call(s32[384]{0:T(512)} %select_reduce_fusion.order_ref, s32[1,128]{1,0:T(1,128)} %get-tuple-element.6.starts_ref, s32[1,128]{1,0:T(1,128)} %get-tuple-element.5.ends_ref, bf16[192,4096]{1,0:T(8,128)(2,1)} %q_ref.1, bf16[192,2048]{1,0:T(8,128)(2,1)} %kv_ref.1), custom_call_target="tpu_custom_call" | custom-call | tf_op jit(solution)/shard_map/attend_and_route/pallas_call | solution.py:401
  106.6 2.7 %copy.9 = bf16[1536,512]{1,0:T(8,128)(2,1)} copy(bf16[1536,512]{1,0:T(8,128)(2,1)} %bitcast.6) | data formatting | bytes 3145728
